TPU v7x, 512 devices: a whole 4x8x8 slice. The times are simulated.
512 devices in a mesh: dp: 32 (over z, y_lo, core), tensor: 16 (over y_hi, x).
Axes of the slice: x: 4, y: 8 (y_hi: 4, y_lo: 2; y = y_hi * 2 + y_lo), z: 8, core: 2. Of those that a mesh axis runs over, the one named last changes fastest.
Arguments:
- tokens: bfloat16 [3072, 8192], P('tensor', 'dp'), may hold values from -6 to 6
- w_gate: bfloat16 [8192, 26624], P('dp', 'tensor'), may hold values from -0.0625 to 0.0625
- gate_pre: bfloat16 [3072, 26624], P('dp', 'tensor'), may hold values from -8 to 8
- up_act: bfloat16 [3072, 26624], P('dp', 'tensor'), may hold values from -6 to 6
- d_hidden: bfloat16 [3072, 26624], P('dp', 'tensor'), may hold values from -6 to 6
- block_mask: int32 [64, 208, 8], P('dp', 'tensor'), may hold values 0 or 1
- lang_ids: int32 [3072], P('tensor'), may hold values from 0 to 7
Outputs:
- input_grad: bfloat16 [3072, 8192], P('tensor', 'dp')
- weight_grad: float32 [8192, 26624], P('dp', 'tensor')
All inputs are finite; a program needn't handle non-finite values. No bound on the sum of `block_mask` on one device may be relied on, other than what follows from the above.
Results may differ from a plain program's by a relative error of at most 0.0049.
Values may be sent and summed in bfloat16 or wider, within the bound.
A program may use at most 128 MiB of HBM per device.

v0:
```python
import jax
import jax.numpy as jnp
from jax import lax
from jax.sharding import PartitionSpec as P


def lookup_masks(language_ids, block_mask):
    language_count = block_mask.shape[2]
    onehot = (language_ids[:, None] == jnp.arange(language_count, dtype=jnp.int32)[None, :]).astype(
        jnp.bfloat16
    )
    table = block_mask.astype(jnp.bfloat16)
    return jnp.einsum("nl,kjl->nkj", onehot, table, preferred_element_type=jnp.float32).astype(
        jnp.bfloat16
    )


def input_rows_of(gradients, mask_rows, w_blocks):
    row_count = gradients.shape[0]
    row_blocks, block_size, col_blocks, _ = w_blocks.shape
    shaped = gradients.reshape(row_count, col_blocks, block_size)

    def input_one_rowblock(block_index):
        mask_part = lax.dynamic_index_in_dim(mask_rows, block_index, 1, keepdims=False)
        scaled = shaped * mask_part[:, :, None]
        w_part = lax.dynamic_index_in_dim(w_blocks, block_index, 0, keepdims=False)
        return jnp.einsum("njf,djf->nd", scaled, w_part, preferred_element_type=jnp.float32)

    parts = lax.map(input_one_rowblock, jnp.arange(row_blocks, dtype=jnp.int32))
    return jnp.transpose(parts, (1, 0, 2)).reshape(row_count, row_blocks * block_size)


def weight_product(row_data, gradients, mask_rows):
    row_count = row_data.shape[0]
    row_blocks = mask_rows.shape[1]
    col_blocks = mask_rows.shape[2]
    block_size = row_data.shape[1] // row_blocks
    shaped = gradients.reshape(row_count, col_blocks, block_size)

    def weight_one_rowblock(block_index):
        mask_part = lax.dynamic_index_in_dim(mask_rows, block_index, 1, keepdims=False)
        scaled = shaped * mask_part[:, :, None]
        data_part = lax.dynamic_slice_in_dim(row_data, block_index * block_size, block_size, 1)
        return jnp.einsum("nd,njf->djf", data_part, scaled, preferred_element_type=jnp.float32)

    parts = lax.map(weight_one_rowblock, jnp.arange(row_blocks, dtype=jnp.int32))
    return parts.reshape(row_blocks * block_size, col_blocks * block_size)


def local(tokens, w_gate, gate_pre, up_act, d_hidden, block_mask, lang_ids):
    gate_value = gate_pre.astype(jnp.float32)
    sigmoid_gate = jax.nn.sigmoid(gate_value)
    gate_grad = (
        d_hidden.astype(jnp.float32)
        * up_act.astype(jnp.float32)
        * sigmoid_gate
        * (1.0 + gate_value * (1.0 - sigmoid_gate))
    ).astype(jnp.bfloat16)
    all_rows, all_ids = (
        lax.all_gather(tokens, "tensor", axis=0, tiled=True),
        lax.all_gather(lang_ids, "tensor", axis=0, tiled=True),
    )
    token_count = all_rows.shape[0]
    row_blocks = block_mask.shape[0]
    col_blocks = block_mask.shape[1]
    block_size = w_gate.shape[0] // row_blocks
    w_blocks = w_gate.reshape(row_blocks, block_size, col_blocks, block_size)
    arrived = lax.all_gather(gate_grad, "dp", axis=0, tiled=True)
    mask_rows = lookup_masks(all_ids, block_mask)
    weights_sum = weight_product(all_rows, arrived, mask_rows)
    updated = input_rows_of(arrived, mask_rows, w_blocks)
    partial_value = updated
    weights_sum, partial_value = (weights_sum, partial_value)
    input_grad = lax.psum_scatter(partial_value, "tensor", scatter_dimension=0, tiled=True)
    weight_grad = weights_sum / jnp.sqrt(jnp.float32(token_count))
    return (input_grad.astype(jnp.bfloat16), weight_grad)


def solution(mesh):
    placed = (
        P("tensor", "dp"),
        P("dp", "tensor"),
        P("dp", "tensor"),
        P("dp", "tensor"),
        P("dp", "tensor"),
        P("dp", "tensor", None),
        P("tensor"),
    )
    return jax.shard_map(
        local,
        mesh=mesh,
        in_specs=placed,
        out_specs=(P("tensor", "dp"), P("dp", "tensor")),
        check_vma=False,
    )
```

profile of v0, /device:TPU:1, one launch (start us, length us, event | category | flops | bytes accessed | tf_op | source)
XLA Modules:
  0.0 261.8 jit_solution(4391563297279748045)
XLA Ops:
  7.2 0.0 copy-start.1
  7.2 0.0 all-gather.3.cloned.1.call-start
  7.2 2.2 fusion.29
  9.4 0.0 all-gather.3.cloned.1.call-update
  9.4 0.0 all-gather.5.cloned.1.call-start
  9.5 0.7 all-gather.5.cloned.1.call-update
  10.2 0.0 reduce-scatter.2.cloned.1.call-start
  10.3 1.3 dynamic-slice
  12.2 0.9 dynamic-update-slice
  13.1 70.2 %all-reduce = s32[3072]{0:T(1024)S(1)} all-reduce(s32[3072]{0:T(1024)S(1)} %dynamic-update-slice), channel_id=1, replica_groups=mesh['dp'=32,'tensor'=16] {'tensor'}, use_global_device_ids=true, to_apply=%add | all-reduce | flops 3072 | bytes 24576
  83.3 1.7 reshape.33
  85.0 1.1 copy.26
  86.2 0.0 copy-done.1
  86.2 0.2 convolution_convert_fusion
  86.4 7.3 %all-gather.3.cloned.1.call-done = bf16[3072,1664]{1,0:T(8,128)(2,1)} async-done(((bf16[96,1664]{1,0:T(8,128)(2,1)}), bf16[3072,1664]{1,0:T(8,128)(2,1)}) %all-gather.3.cloned.1.call-update) | async-done | bytes 10223632 | tf_op jit(solution)/shard_map/all_gather | solution.py:68
  93.7 14.3 %copy.23 = bf16[3072,1664]{0,1:T(8,128)(2,1)} copy(bf16[3072,1664]{1,0:T(8,128)(2,1)} %all-gather.3.cloned.1.call-done) | data formatting | bytes 20447232 | tf_op jit(solution)/shard_map/all_gather | solution.py:68
  108.0 0.0 copy-start
  108.0 14.4 %copy.25 = bf16[3072,13,128]{2,0,1:T(8,128)(2,1)} copy(bf16[3072,13,128]{0,2,1:T(8,128)(2,1)} %bitcast.54) | data formatting | bytes 20447232 | tf_op jit(solution)/shard_map/while | solution.py:29
  122.4 0.0 copy-done
  122.4 25.5 %while.20 = (s32[]{:T(128)}, f32[2,3072,128]{2,1,0:T(8,128)S(1)}, s32[2]{0:T(128)S(1)}, bf16[3072,2,13]{0,2,1:T(8,128)(2,1)S(1)}, bf16[3072,13,128]{2,0,1:T(8,12...) while((s32[]{:T(128)}, f32[2,3072,128]{2,1,0:T(8,128)S(1)}, ...), condition=%wide.region_1.2_spmd, body=%wide.region_0.1_spmd.sunk | while | flops 1313734656 | bytes 12481171 | solution.py:29
  122.4 0.7 dynamic_slice.39
  125.2 9.9 %fusion.43 = f32[2,3072,128]{2,1,0:T(8,128)S(1)} fusion(f32[2,3072,128]{2,1,0:T(8,128)S(1)} %get-tuple-element.204, s32[]{:T(128)} %get-tuple-element.203, bf16[3072,13,128]{2,0,1:T(8,128)(2,1)} %get-tuple-element.216, bf16[3072,13]{0,1:T(8,128)(2,1)S(1)} %dynamic-slice_bitcast_fusion.4, bf16[2,128,13,128]{3,1,2,0:T(8,128)(2,1)} %get-tuple-element.217, ...), kind=kOutput, calls=%fused_computation.4.clone.1 | convolution fusion | flops 1313734656 | bytes 12321284 | tf_op jit(solution)/shard_map/while/body/eval_jaxpr/njf,djf->nd/dot_general | solution.py:27
  135.1 0.7 dynamic_slice.39
  137.9 10.0 %fusion.43 = f32[2,3072,128]{2,1,0:T(8,128)S(1)} fusion(f32[2,3072,128]{2,1,0:T(8,128)S(1)} %get-tuple-element.204, s32[]{:T(128)} %get-tuple-element.203, bf16[3072,13,128]{2,0,1:T(8,128)(2,1)} %get-tuple-element.216, bf16[3072,13]{0,1:T(8,128)(2,1)S(1)} %dynamic-slice_bitcast_fusion.4, bf16[2,128,13,128]{3,1,2,0:T(8,128)(2,1)} %get-tuple-element.217, ...), kind=kOutput, calls=%fused_computation.4.clone.1 | convolution fusion | flops 1313734656 | bytes 12321284 | tf_op jit(solution)/shard_map/while/body/eval_jaxpr/njf,djf->nd/dot_general | solution.py:27
  147.9 2.0 copy_bitcast_fusion
  149.9 0.0 reduce-scatter.2.cloned.1.call-update
  149.9 4.4 %all-gather.5.cloned.1.call-done = bf16[3072,256]{1,0:T(8,128)(2,1)} async-done(((bf16[192,256]{1,0:T(8,128)(2,1)}), bf16[3072,256]{1,0:T(8,128)(2,1)}) %all-gather.5.cloned.1.call-update) | async-done | bytes 1572880 | tf_op jit(solution)/shard_map/all_gather | solution.py:60
  154.4 33.9 %while.21 = (s32[]{:T(128)}, f32[2,128,13,128]{3,1,2,0:T(8,128)S(1)}, s32[2]{0:T(128)S(1)}, bf16[3072,256]{1,0:T(8,128)(2,1)}, bf16[3072,2,13]{0,2,1:T(8,128)(2,...) while((s32[]{:T(128)}, ...), condition=%wide.region_4.5_spmd, body=%wide.region_3.4_spmd.sunk | while | flops 1329070080 | bytes 12120785 | solution.py:46
  154.4 0.6 dynamic_slice.42
  157.6 13.8 %fusion.46 = f32[2,128,13,128]{3,1,2,0:T(8,128)S(1)} fusion(f32[2,128,13,128]{3,1,2,0:T(8,128)S(1)} %get-tuple-element.233, s32[]{:T(128)} %get-tuple-element.232, bf16[3072,13,128]{2,0,1:T(8,128)(2,1)} %get-tuple-element.248, bf16[3072,13]{0,1:T(8,128)(2,1)S(1)} %dynamic-slice_bitcast_fusion.5, bf16[3072,256]{1,0:T(8,128)(2,1)} %get-tuple-element.246, ...), kind=kOutput, calls=%fused_computation.13.clone.1 | convolution fusion | flops 1329070080 | bytes 11960836 | tf_op jit(solution)/shard_map/while/body/eval_jaxpr/nd,njf->djf/dot_general | solution.py:44
  171.3 0.6 dynamic_slice.42
  174.6 13.8 %fusion.46 = f32[2,128,13,128]{3,1,2,0:T(8,128)S(1)} fusion(f32[2,128,13,128]{3,1,2,0:T(8,128)S(1)} %get-tuple-element.233, s32[]{:T(128)} %get-tuple-element.232, bf16[3072,13,128]{2,0,1:T(8,128)(2,1)} %get-tuple-element.248, bf16[3072,13]{0,1:T(8,128)(2,1)S(1)} %dynamic-slice_bitcast_fusion.5, bf16[3072,256]{1,0:T(8,128)(2,1)} %get-tuple-element.246, ...), kind=kOutput, calls=%fused_computation.13.clone.1 | convolution fusion | flops 1329070080 | bytes 11960836 | tf_op jit(solution)/shard_map/while/body/eval_jaxpr/nd,njf->djf/dot_general | solution.py:44
  188.3 0.2 broadcast_multiply_fusion
  188.5 1.0 copy.34
  189.5 1.9 copy.41
  191.4 62.2 %reduce-scatter.2.cloned.1.call-done = f32[192,256]{1,0:T(8,128)} async-done(((f32[3072,256]{1,0:T(8,128)}), f32[192,256]{1,0:T(8,128)}) %reduce-scatter.2.cloned.1.call-update) | async-done | bytes 196624 | tf_op jit(solution)/shard_map/reduce_scatter | solution.py:74
  253.7 1.6 convert_element_type.28
  (9 shorter events, 0.1 us)
Async XLA Ops:
  7.2 79.0 %copy-start.1 = (s32[2,13,8]{1,2,0:T(8,128)S(1)}, s32[2,13,8]{1,2,0:T(8,128)}, u32[]{:S(2)}) copy-start(s32[2,13,8]{1,2,0:T(8,128)} %param.16) | copy-start | bytes 2500
  7.2 86.5 %all-gather.3.cloned.1.call-start = ((), (), s32[]{:S(2)}) async-start(), calls=%async_computation.1 | async-start | bytes 10543104 | tf_op jit(solution)/shard_map/all_gather | solution.py:68
  9.4 144.9 %all-gather.5.cloned.1.call-start = ((), (), s32[]{:S(2)}) async-start(), calls=%async_computation.3 | async-start | bytes 1671168 | tf_op jit(solution)/shard_map/all_gather | solution.py:60
  10.2 243.5 %reduce-scatter.2.cloned.1.call-start = ((), (), s32[]{:S(2)}) async-start(), calls=%async_computation.2 | async-start | bytes 3342336 | tf_op jit(solution)/shard_map/reduce_scatter | solution.py:74
  108.0 14.4 %copy-start = (f32[2,3072,128]{2,1,0:T(8,128)S(1)}, f32[2,3072,128]{2,1,0:T(8,128)}, u32[]{:S(2)}) copy-start(f32[2,3072,128]{2,1,0:T(8,128)} %custom-call) | copy-start | bytes 9437188
Sparse Core Ops, SparseCore 0:
  10.2 83.5 all-gather.2
  96.7 57.6 all-gather.4
  158.6 95.0 reduce-scatter.1
where the time goes:
time: 263 us; the launch traced here: 262 us
  waiting for transfers between devices  74.7 us (28%)
  blocking collectives  70.2 us (27%)
  matrix products  47.7 us (18%)
  local copies, waits for them, and re-layouts  41.2 us (16%)
  between operations  14.5 us (6%)
  loops' own time  9.44 us (4%)
  other arithmetic  3.92 us (1%)
    unnamed x1, blocking collectives  70.2 us
    reduce_scatter x1, waiting for transfers between devices, local(): lax.psum_scatter(partial_value, 'tensor', scatter_dimension=0, tiled=True)  62.2 us
    dot_general x2, matrix products, weight_one_rowblock(): jnp.einsum('nd,njf->djf', data_part, scaled, preferred_element_type=jnp.f...  27.5 us
    dot_general x2, matrix products, input_one_rowblock(): jnp.einsum('njf,djf->nd', scaled, w_part, preferred_element_type=jnp.floa...  19.9 us
    while x2, local copies, waits for them, and re-layouts, input_rows_of(): parts = lax.map(input_one_rowblock, jnp.arange(row_blocks, dtype=jnp.int32))  15.5 us
    all_gather x1, local copies, waits for them, and re-layouts, local(): arrived = lax.all_gather(gate_grad, 'dp', axis=0, tiled=True)  14.3 us
    all_gather x1, waiting for transfers between devices, local(): arrived = lax.all_gather(gate_grad, 'dp', axis=0, tiled=True)  7.28 us
  transfers between devices with their start and end apart: 3, of which 3 were waited for; matrix products, arithmetic and copies ran while one was open for 34% of the time, Pallas kernels for 0%

commit v1 on v0

v1 whole, which is shorter than its diff:
```python
import functools
import math

import jax
import jax.numpy as jnp
from jax import lax
from jax.experimental import pallas as pl
from jax.experimental.pallas import tpu as pltpu
from jax.sharding import PartitionSpec as P

BF = jnp.bfloat16
F32 = jnp.float32
NZ = 8
NX = 4
NH = 4
STAGE_LAG = 3
CONTRACT_ROWS = (((0,), (0,)), ((), ()))
CONTRACT_COLS = (((1,), (1,)), ((), ()))

ROUTES = {
    0: [("up", "all", 1), ("down", "all", 2), ("y", "all", 8)],
    1: [("up", "all", 3), ("y", "all", 9)],
    2: [("down", "all", 4), ("y", "all", 10)],
    3: [("up", "all", 5)],
    4: [("down", "all", 6)],
    5: [("up", "low", 7)],
    6: [("down", "high", 16)],
    7: [],
    8: [],
    9: [("up", "all", 11)],
    10: [("down", "all", 12)],
    11: [("up", "all", 13)],
    12: [("down", "all", 14)],
    13: [("up", "low", 15)],
    14: [("down", "high", 17)],
    15: [],
}
SEND_IDS = {}
for _piece, _sends in ROUTES.items():
    for _n in range(len(_sends)):
        SEND_IDS[(_piece, _n)] = len(SEND_IDS)
N_SENDS = len(SEND_IDS)

EARLY = (8, 3, 4)
AT_STEP = {0: (9, 10), 1: (5, 6), 4: (11, 12), 6: (7,), 9: (13, 14), 13: (15,)}


def kernel(
    rows,
    col_chunks,
    scale,
    packed_ref,
    w_ref,
    gate_ref,
    up_ref,
    dh_ref,
    table_ref,
    out_ref,
    wout_ref,
    grads,
    toks,
    own,
    s1,
    r1,
    s2,
    r2,
    g_send,
    g_recv,
    c_send,
    c_recv,
    t_send,
    t_recv,
    s1_sem,
    r1_sem,
    s2_sem,
    r2_sem,
):
    half = rows // 2
    dp = lax.axis_index("dp")
    tensor = lax.axis_index("tensor")
    core = dp % 2
    y = (dp // 2) % 2
    z = dp // 4
    x = tensor % NX
    yh = tensor // NX

    def dp_of(zz, yy, cc):
        return (zz * 2 + yy) * 2 + cc

    targets = {
        "up": dp_of((z + 1) % NZ, y, core),
        "down": dp_of((z + NZ - 1) % NZ, y, core),
        "y": dp_of(z, 1 - y, core),
        "core": dp_of(z, y, 1 - core),
    }

    def x_peer(step):
        return yh * NX + (x + step) % NX

    def h_peer(step):
        return ((yh + step) % NH) * NX + x

    barrier = pltpu.get_barrier_semaphore()
    for way in ("up", "down", "y", "core"):
        pl.semaphore_signal(
            barrier, inc=1, device_id={"dp": targets[way]}, device_id_type=pl.DeviceIdType.MESH
        )
    for step in range(1, 4):
        for peer in (x_peer(step), h_peer(step)):
            pl.semaphore_signal(
                barrier, inc=1, device_id={"tensor": peer}, device_id_type=pl.DeviceIdType.MESH
            )

    def slot_of(piece):
        r = piece % 8
        dz = ((r + 1) // 2) * (2 * ((r + 1) % 2) - 1)
        return 2 * ((z + dz + NZ) % NZ) + (y + piece // 8) % 2

    def span(part, cc):
        start = cc * half
        if part == "high":
            start = start + half // 2
        return pl.ds(pl.multiple_of(start, 16), half if part == "all" else half // 2)

    def gate_copy(piece, part, way, ssem, rsem):
        view = grads.at[slot_of(piece), span(part, core), :]
        return pltpu.make_async_remote_copy(
            src_ref=view,
            dst_ref=view,
            send_sem=ssem,
            recv_sem=rsem,
            device_id={"dp": targets[way]},
            device_id_type=pl.DeviceIdType.MESH,
        )

    def route_copy(piece, n):
        way, part, rsem = ROUTES[piece][n]
        return gate_copy(piece, part, way, g_send.at[SEND_IDS[(piece, n)]], g_recv.at[rsem])

    def core_copy(piece):
        return gate_copy(piece, "all", "core", c_send.at[piece], c_recv.at[piece])

    def arrived(piece):
        if piece in (7, 15):
            gate_copy(piece, "low", "y", g_send.at[0], g_recv.at[piece]).wait_recv()
            gate_copy(piece, "high", "y", g_send.at[0], g_recv.at[16 + piece // 8]).wait_recv()
        else:
            gate_copy(piece, "all", "y", g_send.at[0], g_recv.at[piece]).wait_recv()

    def pass_on(piece):
        for n in range(len(ROUTES[piece])):
            route_copy(piece, n).start()
        core_copy(piece).start()

    def handle(piece):
        arrived(piece)
        pass_on(piece)

    def tok_copy(src, block, peer, ssem):
        return pltpu.make_async_remote_copy(
            src_ref=src,
            dst_ref=toks.at[block],
            send_sem=ssem,
            recv_sem=t_recv.at[block],
            device_id={"tensor": peer},
            device_id_type=pl.DeviceIdType.MESH,
        )

    def tok_own(n):
        peer = h_peer(n + 1) if n < 3 else x_peer(n - 2)
        return tok_copy(packed_ref, tensor, peer, t_send.at[n])

    def tok_fwd(hstep, xstep):
        block = h_peer(hstep)
        return tok_copy(
            toks.at[block], block, x_peer(xstep), t_send.at[6 + (hstep - 1) * 3 + xstep - 1]
        )

    def tok_arrived(block):
        tok_copy(packed_ref, block, tensor, t_send.at[0]).wait_recv()

    mine = slot_of(0)
    for lo, hi in col_chunks:
        g = gate_ref[:, lo:hi].astype(F32)
        s = jax.nn.sigmoid(g)
        grads[mine, span("all", core), lo:hi] = (
            dh_ref[:, lo:hi].astype(F32) * up_ref[:, lo:hi].astype(F32) * s * (1.0 + g * (1.0 - s))
        ).astype(BF)
    toks[tensor] = packed_ref[...]
    wout_ref[...] = jnp.zeros_like(wout_ref)
    pl.semaphore_wait(barrier, 10)

    pass_on(0)
    for n in range(6):
        tok_own(n).start()
    for hstep in (1, 3):
        tok_arrived(h_peer(hstep))
        for xstep in range(1, 4):
            tok_fwd(hstep, xstep).start()
    for piece in (1, 2):
        handle(piece)
    tok_arrived(h_peer(2))
    for xstep in range(1, 4):
        tok_fwd(2, xstep).start()
    for piece in EARLY:
        handle(piece)
    for xstep in range(1, 4):
        for hstep in range(4):
            tok_arrived(((yh + hstep) % NH) * NX + (x + xstep) % NX)

    def sum_copy(piece, slot):
        return pltpu.make_async_remote_copy(
            src_ref=s1.at[piece],
            dst_ref=r1.at[x * NH + slot // NX],
            send_sem=s1_sem.at[piece],
            recv_sem=r1_sem.at[x * NH + slot // NX],
            device_id={"tensor": yh * NX + slot % NX},
            device_id_type=pl.DeviceIdType.MESH,
        )

    def sum_arrived(index):
        pltpu.make_async_remote_copy(
            src_ref=s1.at[0],
            dst_ref=r1.at[index],
            send_sem=s1_sem.at[0],
            recv_sem=r1_sem.at[index],
            device_id={"tensor": tensor},
            device_id_type=pl.DeviceIdType.MESH,
        ).wait_recv()

    def total_copy(to_h):
        return pltpu.make_async_remote_copy(
            src_ref=s2.at[to_h],
            dst_ref=r2.at[yh],
            send_sem=s2_sem.at[to_h],
            recv_sem=r2_sem.at[yh],
            device_id={"tensor": to_h * NX + x},
            device_id_type=pl.DeviceIdType.MESH,
        )

    def step_body(step, carry):
        for at, pieces in AT_STEP.items():

            @pl.when(step == at)
            def _():
                for piece in pieces:
                    handle(piece)

        @pl.when(step < 16)
        def _():
            slot = slot_of(step)
            other = grads.at[slot, span("all", 1 - core), :]
            pltpu.make_async_remote_copy(
                src_ref=other,
                dst_ref=other,
                send_sem=c_send.at[0],
                recv_sem=c_recv.at[step],
                device_id={"dp": targets["core"]},
                device_id_type=pl.DeviceIdType.MESH,
            ).wait_recv()
            onehot = toks[slot, rows:, :rows]
            parts = []
            for a in range(2):
                data = toks[slot, :rows, a * 128 : (a + 1) * 128]
                part = None
                for lo, hi in col_chunks:
                    mask = lax.dot_general(
                        onehot, table_ref[a, :, lo:hi], CONTRACT_ROWS, preferred_element_type=F32
                    )
                    scaled = grads[slot, :, lo:hi] * mask.astype(BF)
                    term = lax.dot_general(
                        scaled,
                        w_ref[a * 128 : (a + 1) * 128, lo:hi],
                        CONTRACT_COLS,
                        preferred_element_type=F32,
                    )
                    part = term if part is None else part + term
                    wout_ref[a * 128 : (a + 1) * 128, lo:hi] += lax.dot_general(
                        data, scaled, CONTRACT_ROWS, preferred_element_type=F32
                    )
                parts.append(part)
            part = jnp.concatenate(parts, axis=1)

            @pl.when(slot % NX == x)
            def _():
                own[slot // NX] = part

            @pl.when(slot % NX != x)
            def _():
                s1[step] = part.astype(BF)
                sum_copy(step, slot).start()

        @pl.when(step >= STAGE_LAG)
        def _():
            slot = slot_of(step - STAGE_LAG)
            to_h = slot // NX

            @pl.when(slot % NX == x)
            def _():
                total = own[to_h]
                for xstep in range(1, 4):
                    index = ((x + xstep) % NX) * NH + to_h
                    sum_arrived(index)
                    total = total + r1[index].astype(F32)

                @pl.when(to_h == yh)
                def _():
                    own[to_h] = total

                @pl.when(to_h != yh)
                def _():
                    s2[to_h] = total.astype(BF)
                    total_copy(to_h).start()

        return carry

    lax.fori_loop(0, 16 + STAGE_LAG, step_body, 0)

    wout_ref[...] = wout_ref[...] * scale

    total = own[yh]
    for hstep in range(1, 4):
        src = (yh + hstep) % NH
        pltpu.make_async_remote_copy(
            src_ref=s2.at[0],
            dst_ref=r2.at[src],
            send_sem=s2_sem.at[0],
            recv_sem=r2_sem.at[src],
            device_id={"tensor": tensor},
            device_id_type=pl.DeviceIdType.MESH,
        ).wait_recv()
        total = total + r2[src].astype(F32)
    out_ref[...] = total.astype(BF)

    for piece in range(16):
        for n in range(len(ROUTES[piece])):
            route_copy(piece, n).wait_send()
        core_copy(piece).wait_send()
    for n in range(6):
        tok_own(n).wait_send()
    for hstep in range(1, 4):
        for xstep in range(1, 4):
            tok_fwd(hstep, xstep).wait_send()
        total_copy((yh + hstep) % NH).wait_send()

    def drain(step, carry):
        slot = slot_of(step)

        @pl.when(slot % NX != x)
        def _():
            sum_copy(step, slot).wait_send()

        return carry

    lax.fori_loop(0, 16, drain, 0)


def local(tokens, w_gate, gate_pre, up_act, d_hidden, block_mask, lang_ids):
    rows, width = tokens.shape
    hidden = w_gate.shape[1]
    row_blocks, col_blocks, langs = block_mask.shape
    table = jnp.broadcast_to(
        jnp.transpose(block_mask.astype(BF), (0, 2, 1))[:, :, :, None],
        (row_blocks, langs, col_blocks, hidden // col_blocks),
    ).reshape(row_blocks, langs, hidden)
    table = jnp.pad(table, ((0, 0), (0, 16 - langs), (0, 0)))
    onehot = (lang_ids[None, :] == jnp.arange(16, dtype=jnp.int32)[:, None]).astype(BF)
    packed = jnp.concatenate([tokens, jnp.pad(onehot, ((0, 0), (0, width - rows)))], axis=0)
    col_chunks = ((0, 512), (512, 1024), (1024, hidden))
    dma = pltpu.SemaphoreType.DMA
    vmem = pl.BlockSpec(memory_space=pltpu.VMEM)
    return tuple(
        pl.pallas_call(
            functools.partial(kernel, rows, col_chunks, 1.0 / math.sqrt(16 * rows)),
            out_shape=(
                jax.ShapeDtypeStruct((rows, width), BF),
                jax.ShapeDtypeStruct((width, hidden), F32),
            ),
            in_specs=[vmem] * 6,
            out_specs=(vmem, vmem),
            scratch_shapes=[
                pltpu.VMEM((16, rows, hidden), BF),
                pltpu.VMEM((16, rows + 16, width), BF),
                pltpu.VMEM((NH, rows, width), F32),
                pltpu.VMEM((16, rows, width), BF),
                pltpu.VMEM((16, rows, width), BF),
                pltpu.VMEM((NH, rows, width), BF),
                pltpu.VMEM((NH, rows, width), BF),
                dma((N_SENDS,)),
                dma((18,)),
                dma((16,)),
                dma((16,)),
                dma((15,)),
                dma((16,)),
                dma((16,)),
                dma((16,)),
                dma((NH,)),
                dma((NH,)),
            ],
            compiler_params=pltpu.CompilerParams(collective_id=0, has_side_effects=True),
        )(packed, w_gate, gate_pre, up_act, d_hidden, table)
    )


def solution(mesh):
    placed = (
        P("tensor", "dp"),
        P("dp", "tensor"),
        P("dp", "tensor"),
        P("dp", "tensor"),
        P("dp", "tensor"),
        P("dp", "tensor", None),
        P("tensor"),
    )
    return jax.shard_map(
        local,
        mesh=mesh,
        in_specs=placed,
        out_specs=(P("tensor", "dp"), P("dp", "tensor")),
        check_vma=False,
    )
```

time: 263 us -> 107 us (0.41)
  the two profiles are of different devices: /device:TPU:1 before, /device:TPU:108 now
where the time goes in v1:
time: 107 us
  Pallas kernels  98 us (92%)
  local copies, waits for them, and re-layouts  5.12 us (5%)
  other arithmetic  2.95 us (3%)
    pallas_call x1, Pallas kernels, local(): pl.pallas_call(functools.partial(kernel, rows, col_chunks, 1.0 / math.sqr...  98 us
    unnamed x2, local copies, waits for them, and re-layouts  4.29 us

profile of v1, /device:TPU:108, one launch (start us, length us, event | category | flops | bytes accessed | tf_op | source)
XLA Modules:
  0.0 106.7 jit_solution(12219969556762878745)
XLA Ops:
  0.6 0.7 convert_bitcast_fusion
  1.3 0.1 copy.9
  1.4 0.7 iota_compare_fusion
  2.1 0.1 broadcast_bitcast_fusion
  2.2 0.7 pad.13.table_ref
  2.9 1.5 %pad_maximum_fusion.packed_ref = bf16[208,256]{1,0:T(8,128)(2,1)} fusion(bf16[16,256]{1,0:T(8,128)(2,1)S(1)} %pad_convert_fusion, bf16[192,256]{1,0:T(8,128)(2,1)} %param.7), kind=kLoop, calls=%fused_computation | loop fusion | flops 212992 | bytes 212992 | tf_op jit(solution)/shard_map/concatenate | solution.py:368
  4.4 98.0 %shard_map.86 = (bf16[192,256]{1,0:T(8,128)(2,1)}, f32[256,1664]{1,0:T(8,128)}) custom-call(bf16[208,256]{1,0:T(8,128)(2,1)} %pad_maximum_fusion.packed_ref, bf16[256,1664]{1,0:T(8,128)(2,1)} %w_ref.1, bf16[96,1664]{1,0:T(8,128)(2,1)} %gate_ref.1, bf16[96,1664]{1,0:T(8,128)(2,1)} %up_ref.1, bf16[96,1664]{1,0:T(8,128)(2,1)} %dh_ref.1, ...), custom_call_target="tpu_custom_call" | custom-call | tf_op jit(solution)/shard_map/pallas_call | solution.py:373
  102.4 1.5 %copy.12 = bf16[192,256]{1,0:T(8,128)(2,1)} copy(bf16[192,256]{1,0:T(8,128)(2,1)} %get-tuple-element.4) | data formatting | bytes 196608
  103.9 2.7 %copy.13 = f32[256,1664]{1,0:T(8,128)} copy(f32[256,1664]{1,0:T(8,128)} %get-tuple-element.5) | data formatting | bytes 3407872
  (1 shorter events, 0.0 us)

commit v2 on v1

v2 whole, which is shorter than its diff:
```python
import functools
import math

import jax
import jax.numpy as jnp
from jax import lax
from jax.experimental import pallas as pl
from jax.experimental.pallas import tpu as pltpu
from jax.sharding import PartitionSpec as P

BF = jnp.bfloat16
F32 = jnp.float32
NZ = 8
NX = 4
NH = 4
STAGE_LAG = 3
CONTRACT_ROWS = (((0,), (0,)), ((), ()))
CONTRACT_COLS = (((1,), (1,)), ((), ()))

ROUTES = {(piece, h): [] for piece in range(16) for h in range(2)}
for _h in range(2):
    ROUTES[0, _h] = [("up", 1), ("down", 2), ("y", 8)]
    ROUTES[1, _h] = [("up", 3), ("y", 9)]
    ROUTES[2, _h] = [("down", 4), ("y", 10)]
    for _p in (3, 9, 11):
        ROUTES[_p, _h] = [("up", _p + 2)]
    for _p in (4, 10, 12):
        ROUTES[_p, _h] = [("down", _p + 2)]
ROUTES[5, 0] = [("up", 7)]
ROUTES[6, 1] = [("down", 7)]
ROUTES[13, 0] = [("up", 15)]
ROUTES[14, 1] = [("down", 15)]
SENDS = [(piece, h, way, to) for (piece, h), way_to in ROUTES.items() for way, to in way_to]
SEND_ID = {(piece, h, way): n for n, (piece, h, way, _) in enumerate(SENDS)}
N_SENDS = len(SENDS)


AT_STEP = {
    1: ((5, 0), (6, 0)),
    3: ((5, 1), (6, 1), (9, 0), (10, 0)),
    4: ((9, 1), (10, 1)),
    6: ((7, 0), (7, 1)),
    7: ((8, 0), (8, 1)),
    9: ((11, 0), (12, 0)),
    10: ((11, 1), (12, 1)),
    12: ((13, 0), (14, 0)),
    13: ((13, 1), (14, 1)),
    15: ((15, 0), (15, 1)),
}


def kernel(
    rows,
    col_chunks,
    tok_ref,
    ids_ref,
    bits_ref,
    w_ref,
    gate_ref,
    up_ref,
    dh_ref,
    out_ref,
    wout_ref,
    table_ref,
    grads,
    toks,
    own,
    s1,
    r1,
    s2,
    r2,
    g_send,
    g_recv,
    c_send,
    c_recv,
    t_send,
    t_recv,
    s1_sem,
    r1_sem,
    s2_sem,
    r2_sem,
):
    half = rows // 2
    dp = lax.axis_index("dp")
    tensor = lax.axis_index("tensor")
    core = dp % 2
    y = (dp // 2) % 2
    z = dp // 4
    x = tensor % NX
    yh = tensor // NX

    def dp_of(zz, yy, cc):
        return (zz * 2 + yy) * 2 + cc

    targets = {
        "up": dp_of((z + 1) % NZ, y, core),
        "down": dp_of((z + NZ - 1) % NZ, y, core),
        "y": dp_of(z, 1 - y, core),
        "core": dp_of(z, y, 1 - core),
    }

    def x_peer(step):
        return yh * NX + (x + step) % NX

    def h_peer(step):
        return ((yh + step) % NH) * NX + x

    barrier = pltpu.get_barrier_semaphore()
    for way in ("up", "down", "y", "core"):
        pl.semaphore_signal(
            barrier, inc=1, device_id={"dp": targets[way]}, device_id_type=pl.DeviceIdType.MESH
        )
    for step in range(1, 4):
        for peer in (x_peer(step), h_peer(step)):
            pl.semaphore_signal(
                barrier, inc=1, device_id={"tensor": peer}, device_id_type=pl.DeviceIdType.MESH
            )

    def slot_of(piece):
        r = piece % 8
        dz = ((r + 1) // 2) * (2 * ((r + 1) % 2) - 1)
        return 2 * ((z + dz + NZ) % NZ) + (y + piece // 8) % 2

    def span(h, cc):
        start = cc * half if h is None else cc * half + h * (half // 2)
        return pl.ds(pl.multiple_of(start, 16), half if h is None else half // 2)

    def gate_copy(piece, h, way, ssem, rsem):
        view = grads.at[slot_of(piece), span(h, core), :]
        return pltpu.make_async_remote_copy(
            src_ref=view,
            dst_ref=view,
            send_sem=ssem,
            recv_sem=rsem,
            device_id={"dp": targets[way]},
            device_id_type=pl.DeviceIdType.MESH,
        )

    def route_copy(piece, h, way, to):
        return gate_copy(piece, h, way, g_send.at[SEND_ID[piece, h, way]], g_recv.at[2 * to + h])

    def core_copy(piece):
        return gate_copy(piece, None, "core", c_send.at[piece], c_recv.at[piece])

    def pass_on(piece, h, ways=("up", "down", "y")):
        for way, to in ROUTES[piece, h]:
            if way in ways:
                route_copy(piece, h, way, to).start()

    def handle(piece, h):
        gate_copy(piece, h, "y", g_send.at[0], g_recv.at[2 * piece + h]).wait_recv()
        pass_on(piece, h)
        if h == 1:
            core_copy(piece).start()

    def tok_copy(block, part, peer, ssem):
        view = toks.at[block]
        if part is not None:
            view = toks.at[block, pl.ds(112 * part, 112 - 16 * part), :]
        return pltpu.make_async_remote_copy(
            src_ref=view,
            dst_ref=view,
            send_sem=ssem,
            recv_sem=t_recv.at[block + 16 * (part or 0)],
            device_id={"tensor": peer},
            device_id_type=pl.DeviceIdType.MESH,
        )

    def block_at(hstep, xstep):
        return ((yh + hstep) % NH) * NX + (x + xstep) % NX

    tok_sends = []
    for side in (1, 3):
        tok_sends.append((0, 0, None, side, 0))
        tok_sends.append((0, 0, None, 0, side))
    for hstep in range(4):
        for side, part in ((3, 0), (1, 1)):
            tok_sends.append((hstep, side, part, 0, 4 - side))
    for hstep in (1, 2, 3):
        for side in (1, 3):
            tok_sends.append((hstep, 0, None, 0, side))
    for side, part in ((3, 0), (1, 1)):
        tok_sends.append((side, 0, part, 4 - side, 0))

    def tok_send(send):
        hstep, xstep, part, to_h, to_x = send
        return tok_copy(
            block_at(hstep, xstep), part, block_at(to_h, to_x), t_send.at[tok_sends.index(send)]
        )

    def tok_arrived(hstep, xstep):
        block = block_at(hstep, xstep)
        if hstep == 2 and xstep == 0 or xstep == 2:
            tok_copy(block, 0, tensor, t_send.at[0]).wait_recv()
            tok_copy(block, 1, tensor, t_send.at[0]).wait_recv()
        else:
            tok_copy(block, None, tensor, t_send.at[0]).wait_recv()

    def tok_handle(hstep, xstep):
        if (hstep, xstep) != (0, 0):
            tok_arrived(hstep, xstep)
        for send in tok_sends:
            if send[:2] == (hstep, xstep):
                tok_send(send).start()

    count = ids_ref.shape[1]
    toks[tensor, :rows, :] = tok_ref[...]
    row = lax.broadcasted_iota(jnp.int32, (16, count), 0)
    same = jnp.where(row == ids_ref[...], 1.0, 0.0).astype(BF)
    toks[tensor, rows:, :count] = same
    mine = slot_of(0)
    for lo, hi in col_chunks:
        g = gate_ref[:, lo:hi].astype(F32)
        s = jax.nn.sigmoid(g)
        grads[mine, span(None, core), lo:hi] = (
            dh_ref[:, lo:hi].astype(F32) * up_ref[:, lo:hi].astype(F32) * s * (1.0 + g * (1.0 - s))
        ).astype(BF)
    pl.semaphore_wait(barrier, 10)

    tok_handle(0, 0)
    pass_on(0, 0, ("up", "down"))
    pass_on(0, 1, ("up", "down"))
    core_copy(0).start()

    hidden = wout_ref.shape[1]
    langs, col_blocks = bits_ref.shape[1:]
    lane = lax.broadcasted_iota(jnp.int32, (col_blocks, hidden), 1)
    first = lax.broadcasted_iota(jnp.int32, (col_blocks, hidden), 0) * 128
    spread = jnp.where((lane >= first) & (lane < first + 128), 1.0, 0.0).astype(BF)
    for a in range(2):
        bits = bits_ref[a].astype(F32).astype(BF)
        wide = jnp.dot(bits, spread, preferred_element_type=F32)
        table_ref[a] = jnp.concatenate([wide, jnp.zeros((16 - langs, hidden), F32)], axis=0).astype(BF)
    wout_ref[...] = jnp.zeros_like(wout_ref)

    tok_handle(0, 1)
    tok_handle(0, 3)
    handle(1, 0)
    handle(2, 0)
    tok_handle(1, 0)
    tok_handle(3, 0)
    handle(1, 1)
    handle(2, 1)
    pass_on(0, 0, ("y",))
    pass_on(0, 1, ("y",))
    for side in (1, 3):
        tok_handle(1, side)
        tok_handle(3, side)
    handle(3, 0)
    handle(4, 0)
    tok_handle(2, 0)
    handle(3, 1)
    handle(4, 1)
    tok_handle(2, 1)
    tok_handle(2, 3)

    def sum_copy(piece, slot):
        return pltpu.make_async_remote_copy(
            src_ref=s1.at[piece],
            dst_ref=r1.at[x * NH + slot // NX],
            send_sem=s1_sem.at[piece],
            recv_sem=r1_sem.at[x * NH + slot // NX],
            device_id={"tensor": yh * NX + slot % NX},
            device_id_type=pl.DeviceIdType.MESH,
        )

    def sum_arrived(index):
        pltpu.make_async_remote_copy(
            src_ref=s1.at[0],
            dst_ref=r1.at[index],
            send_sem=s1_sem.at[0],
            recv_sem=r1_sem.at[index],
            device_id={"tensor": tensor},
            device_id_type=pl.DeviceIdType.MESH,
        ).wait_recv()

    def total_copy(to_h):
        return pltpu.make_async_remote_copy(
            src_ref=s2.at[to_h],
            dst_ref=r2.at[yh],
            send_sem=s2_sem.at[to_h],
            recv_sem=r2_sem.at[yh],
            device_id={"tensor": to_h * NX + x},
            device_id_type=pl.DeviceIdType.MESH,
        )

    def step_body(step, carry):
        for at, pieces in AT_STEP.items():

            @pl.when(step == at)
            def _():
                for piece, h in pieces:
                    handle(piece, h)

        @pl.when(step < 16)
        def _():
            slot = slot_of(step)
            other = grads.at[slot, span(None, 1 - core), :]
            pltpu.make_async_remote_copy(
                src_ref=other,
                dst_ref=other,
                send_sem=c_send.at[0],
                recv_sem=c_recv.at[step],
                device_id={"dp": targets["core"]},
                device_id_type=pl.DeviceIdType.MESH,
            ).wait_recv()

            @pl.when((slot + NX - x) % NX == 2)
            def _():
                tok_copy(slot, 0, tensor, t_send.at[0]).wait_recv()
                tok_copy(slot, 1, tensor, t_send.at[0]).wait_recv()

            onehot = toks[slot, rows:, :rows]
            parts = []
            for a in range(2):
                data = toks[slot, :rows, a * 128 : (a + 1) * 128]
                part = None
                for lo, hi in col_chunks:
                    mask = lax.dot_general(
                        onehot, table_ref[a, :, lo:hi], CONTRACT_ROWS, preferred_element_type=F32
                    )
                    scaled = grads[slot, :, lo:hi] * mask.astype(BF)
                    term = lax.dot_general(
                        scaled,
                        w_ref[a * 128 : (a + 1) * 128, lo:hi],
                        CONTRACT_COLS,
                        preferred_element_type=F32,
                    )
                    part = term if part is None else part + term
                    wout_ref[a * 128 : (a + 1) * 128, lo:hi] += lax.dot_general(
                        data, scaled, CONTRACT_ROWS, preferred_element_type=F32
                    )
                parts.append(part)
            part = jnp.concatenate(parts, axis=1)

            @pl.when(slot % NX == x)
            def _():
                own[slot // NX] = part

            @pl.when(slot % NX != x)
            def _():
                s1[step] = part.astype(BF)
                sum_copy(step, slot).start()

        @pl.when(step >= STAGE_LAG)
        def _():
            slot = slot_of(step - STAGE_LAG)
            to_h = slot // NX

            @pl.when(slot % NX == x)
            def _():
                total = own[to_h]
                for xstep in range(1, 4):
                    index = ((x + xstep) % NX) * NH + to_h
                    sum_arrived(index)
                    total = total + r1[index].astype(F32)

                @pl.when(to_h == yh)
                def _():
                    own[to_h] = total

                @pl.when(to_h != yh)
                def _():
                    s2[to_h] = total.astype(BF)
                    total_copy(to_h).start()

        return carry

    lax.fori_loop(0, 16 + STAGE_LAG, step_body, 0)

    total = own[yh]
    for hstep in range(1, 4):
        src = (yh + hstep) % NH
        pltpu.make_async_remote_copy(
            src_ref=s2.at[0],
            dst_ref=r2.at[src],
            send_sem=s2_sem.at[0],
            recv_sem=r2_sem.at[src],
            device_id={"tensor": tensor},
            device_id_type=pl.DeviceIdType.MESH,
        ).wait_recv()
        total = total + r2[src].astype(F32)
    out_ref[...] = total.astype(BF)

    for send in SENDS:
        route_copy(*send).wait_send()
    for piece in range(16):
        core_copy(piece).wait_send()
    for send in tok_sends:
        tok_send(send).wait_send()
    for hstep in range(1, 4):
        total_copy((yh + hstep) % NH).wait_send()

    def drain(step, carry):
        slot = slot_of(step)

        @pl.when(slot % NX != x)
        def _():
            sum_copy(step, slot).wait_send()

        return carry

    lax.fori_loop(0, 16, drain, 0)


def local(tokens, w_gate, gate_pre, up_act, d_hidden, block_mask, lang_ids):
    rows, width = tokens.shape
    hidden = w_gate.shape[1]
    ids = lang_ids.reshape(1, rows)
    bits = jnp.transpose(block_mask, (0, 2, 1))
    col_chunks = ((0, 512), (512, 1024), (1024, hidden))
    dma = pltpu.SemaphoreType.DMA
    vmem = pl.BlockSpec(memory_space=pltpu.VMEM)
    input_grad, weights_sum = pl.pallas_call(
        functools.partial(kernel, rows, col_chunks),
        out_shape=(
            jax.ShapeDtypeStruct((rows, width), BF),
            jax.ShapeDtypeStruct((width, hidden), F32),
        ),
        in_specs=[vmem] * 7,
        out_specs=(vmem, vmem),
        scratch_shapes=[
            pltpu.VMEM((2, 16, hidden), BF),
            pltpu.VMEM((16, rows, hidden), BF),
            pltpu.VMEM((16, rows + 16, width), BF),
            pltpu.VMEM((NH, rows, width), F32),
            pltpu.VMEM((16, rows, width), BF),
            pltpu.VMEM((16, rows, width), BF),
            pltpu.VMEM((NH, rows, width), BF),
            pltpu.VMEM((NH, rows, width), BF),
            dma((N_SENDS,)),
            dma((32,)),
            dma((16,)),
            dma((16,)),
            dma((20,)),
            dma((32,)),
            dma((16,)),
            dma((16,)),
            dma((NH,)),
            dma((NH,)),
        ],
        compiler_params=pltpu.CompilerParams(collective_id=0, has_side_effects=True),
    )(tokens, ids, bits, w_gate, gate_pre, up_act, d_hidden)
    return input_grad, weights_sum * (1.0 / math.sqrt(16 * rows))


def solution(mesh):
    placed = (
        P("tensor", "dp"),
        P("dp", "tensor"),
        P("dp", "tensor"),
        P("dp", "tensor"),
        P("dp", "tensor"),
        P("dp", "tensor", None),
        P("tensor"),
    )
    return jax.shard_map(
        local,
        mesh=mesh,
        in_specs=placed,
        out_specs=(P("tensor", "dp"), P("dp", "tensor")),
        check_vma=False,
    )
```

time: 107 us -> 93.3 us (0.87)
  the two profiles are of different devices: /device:TPU:108 before, /device:TPU:22 now
where the time goes in v2:
time: 93.3 us; the launch traced here: 93.1 us
  Pallas kernels  89 us (95%)
  other arithmetic  2.82 us (3%)
    pallas_call x1, Pallas kernels, local(): pl.pallas_call(functools.partial(kernel, rows, col_chunks), out_shape=(ja...  89 us
    mul x1, other arithmetic, local(): return (input_grad, weights_sum * (1.0 / math.sqrt(16 * rows)))  2.82 us

profile of v2, /device:TPU:22, one launch (start us, length us, event | category | flops | bytes accessed | tf_op | source)
XLA Modules:
  0.0 93.1 jit_solution(17785332994429031551)
XLA Ops:
  0.6 89.0 %shard_map.86 = (bf16[192,256]{1,0:T(8,128)(2,1)}, f32[256,1664]{1,0:T(8,128)}) custom-call(bf16[192,256]{1,0:T(8,128)(2,1)} %tok_ref.1, s32[1,192]{1,0:T(1,128)} %bitcast.3, s32[2,8,13]{2,1,0:T(8,128)} %bitcast.2, bf16[256,1664]{1,0:T(8,128)(2,1)} %w_ref.1, bf16[96,1664]{1,0:T(8,128)(2,1)} %gate_ref.1, bf16[96,1664]{1,0:T(8,128)(2,1)} %up_ref.1, ...), custom_call_target="tpu_custom_call" | custom-call | tf_op jit(solution)/shard_map/pallas_call | solution.py:414
  89.6 0.0 copy-start
  89.7 2.8 %broadcast_multiply_fusion = f32[256,1664]{1,0:T(8,128)} fusion(f32[256,1664]{1,0:T(8,128)} %get-tuple-element.5), kind=kLoop, calls=%fused_computation | loop fusion | flops 425984 | bytes 3407872 | tf_op jit(solution)/shard_map/mul | solution.py:444
  92.5 0.0 copy-done
  92.5 0.6 copy.10
Async XLA Ops:
  89.6 2.8 %copy-start = (bf16[192,256]{1,0:T(8,128)(2,1)S(1)}, bf16[192,256]{1,0:T(8,128)(2,1)}, u32[]{:S(2)}) copy-start(bf16[192,256]{1,0:T(8,128)(2,1)} %get-tuple-element.8) | copy-start | bytes 294916
